TPU v7x, 256 devices: a whole 4x4x8 slice. The times are simulated.
256 devices in a mesh: slab: 64 (over y, z, core), layer: 4 (over x).
Axes of the slice: x: 4, y: 4, z: 8, core: 2. Of those that a mesh axis runs over, the one named last changes fastest.
Arguments:
- hamilton_blocks: bfloat16 [1024, 128, 128], P(('slab', 'layer')), may hold values from -0.25 to 0.25
- pair_ids: int32 [256, 10], P(('slab', 'layer')), may hold values from 0 to 1023, as said below
- weights: float32 [256, 10], P(('slab', 'layer')), may hold values from 0.25 to 4
- potential: float32 [1], replicated, may hold values from -1 to 1
Outputs:
- density: float32 [1024, 128, 128], P(('slab', 'layer'))
- energy: float32 [1024, 128, 128], P(('slab', 'layer'))
Inputs may be any that keep to these rules, and one draw needn't show every extreme that they name: `pair_ids`: the entries of one row are distinct. Slot p is owned by device p // 4, whose slab index is that device // 4 and layer index that device % 4. Row d names only slots owned by devices whose slab index is that of device d, or one more or one less cyclically over 64, with any layer index. A row names at most 4 slots of any one device, and exactly 4 of some device; in every draw some device has exactly 4 of its slots named by each of the 3 * 4 rows that may name its slots.
All inputs are finite; a program needn't handle non-finite values.
Results may differ from a plain program's by a relative error of at most 0.0017.
Values may be sent and summed in bfloat16 or wider, within the bound.
A program may use at most 64 MiB of HBM per device.

v0:
```python
import jax
import jax.numpy as jnp
import numpy as np
from jax import lax
from jax.sharding import PartitionSpec as P

BS = 128
NB = 4
ITERS = 2


def with_halo(cells, sides, width):
    for axis, dim in sides:
        count = lax.axis_size(axis)
        head = lax.slice_in_dim(cells, 0, width, axis=dim)
        tail = lax.slice_in_dim(cells, cells.shape[dim] - width, cells.shape[dim], axis=dim)
        cells = jnp.concatenate(
            [
                lax.ppermute(tail, axis, [(i, (i + 1) % count) for i in range(count)]),
                cells,
                lax.ppermute(head, axis, [((i + 1) % count, i) for i in range(count)]),
            ],
            axis=dim,
        )
    return cells


def submatrix_step(blocks, weight_row, mu_value):
    block_rows, block_cols = np.triu_indices(NB)
    block_rows = block_rows.astype(np.int32)
    block_cols = block_cols.astype(np.int32)
    upper_grid = (
        jnp.zeros((NB, NB, BS, BS), jnp.float32)
        .at[block_rows, block_cols]
        .set(blocks.astype(jnp.float32))
    )
    sub_order = NB * BS
    upper = upper_grid.transpose(0, 2, 1, 3).reshape(sub_order, sub_order)
    hamilt = upper + upper.T
    identity = jnp.eye(sub_order, dtype=jnp.float32)
    shifted = mu_value * identity - hamilt
    norm_scale = 2.0 * jnp.sqrt(jnp.sum(shifted * shifted) / sub_order + 1e-06)
    iterate = shifted / norm_scale
    for iteration in range(ITERS):
        square = jnp.dot(
            iterate, iterate, precision=lax.Precision.HIGHEST, preferred_element_type=jnp.float32
        )
        iterate = 1.5 * iterate - 0.5 * jnp.dot(
            iterate, square, precision=lax.Precision.HIGHEST, preferred_element_type=jnp.float32
        )
    dens_sub = 0.5 * (identity + iterate)
    energy_sub = jnp.dot(
        dens_sub, hamilt, precision=lax.Precision.HIGHEST, preferred_element_type=jnp.float32
    )
    dens_pairs = dens_sub.reshape(NB, BS, NB, BS).transpose(0, 2, 1, 3)[block_rows, block_cols]
    energy_pairs = energy_sub.reshape(NB, BS, NB, BS).transpose(0, 2, 1, 3)[block_rows, block_cols]
    scaled = weight_row[:, None, None]
    return (
        (scaled * dens_pairs).astype(jnp.bfloat16),
        (scaled * energy_pairs).astype(jnp.bfloat16),
    )


def shards(hamilton_blocks, pair_ids, weights, potential):
    pieces = hamilton_blocks.shape[0]
    layer_count = lax.axis_size("layer")
    slab_count = lax.axis_size("slab")
    here_slab = lax.axis_index("slab")
    here_layer = lax.axis_index("layer")
    requests = pair_ids[0]
    owner_device = requests // pieces
    owner_slab = owner_device // layer_count
    owner_layer = owner_device % layer_count
    owner_slot = requests % pieces
    offset = (owner_slab - here_slab + 1 + slab_count) % slab_count
    table_index = (offset * layer_count + owner_layer) * pieces + owner_slot
    flat_size = BS * BS
    column = lax.all_gather(hamilton_blocks, "layer", axis=0, tiled=True)
    nearby = with_halo(column, (("slab", 0),), layer_count * pieces)
    blocks = nearby[table_index]
    dens_parts, energy_parts = submatrix_step(blocks, weights[0], potential[0])
    stacked = jnp.stack([dens_parts, energy_parts])
    part_count = stacked.shape[1]
    column_parts, column_ids = (
        lax.all_gather(stacked, "layer", axis=1, tiled=True),
        lax.all_gather(requests, "layer", axis=0, tiled=True),
    )
    near_parts = with_halo(column_parts, (("slab", 1),), layer_count * part_count)
    near_ids = with_halo(column_ids, (("slab", 0),), layer_count * part_count)
    own_pairs = (here_slab * layer_count + here_layer) * pieces + jnp.arange(
        pieces, dtype=jnp.int32
    )
    match_table = (near_ids[None, :] == own_pairs[:, None]).astype(jnp.bfloat16)
    flat = near_parts.reshape(2, near_parts.shape[1], flat_size)
    summed = jnp.einsum("pk,gkf->gpf", match_table, flat, preferred_element_type=jnp.float32)
    totals_all = summed.reshape(2, pieces, BS, BS)
    return (totals_all[0], totals_all[1])


def solution(mesh):
    placed = (
        P(("slab", "layer"), None, None),
        P(("slab", "layer"), None),
        P(("slab", "layer"), None),
        P(),
    )
    return jax.shard_map(
        shards,
        mesh=mesh,
        in_specs=placed,
        out_specs=(P(("slab", "layer"), None, None), P(("slab", "layer"), None, None)),
        check_vma=False,
    )
```

profile of v0, /device:TPU:2, one launch (start us, length us, event | category | flops | bytes accessed | tf_op | source)
XLA Modules:
  0.0 159.9 jit_solution(1452712038793661266)
XLA Ops:
  7.2 13.7 %all_gather.9 = bf16[16,128,128]{2,1,0:T(8,128)(2,1)S(1)} all-gather(bf16[4,128,128]{2,1,0:T(8,128)(2,1)} %param.12), channel_id=1, replica_groups=mesh['slab'=64,'layer'=4] {'layer'}, dimensions={0}, use_global_device_ids=true | all-gather | bytes 655360 | tf_op jit(solution)/shard_map/all_gather | solution.py:78
  20.9 4.2 %collective-permute-start.1 = (bf16[16,128,128]{2,1,0:T(8,128)(2,1)S(1)}, bf16[16,128,128]{2,1,0:T(8,128)(2,1)S(1)}, u32[]{:S(2)}, u32[]{:S(2)}) collective-permute-start(bf16[16,128,128]{2,1,0:T(8,128)(2,1)S(1)} %all_gather.9), channel_id=1, source_target_pairs={{4,0},{8,4},{12,8},{16,12},{20,16},{24,20},{28,24},{32,28},{36,32}... | collective-permute-start | bytes 1572872 | tf_op jit(solution)/shard_map/ppermute | solution.py:21
  25.8 0.7 fusion.18
  26.5 5.3 %collective-permute-done.1 = bf16[16,128,128]{2,1,0:T(8,128)(2,1)S(1)} collective-permute-done((bf16[16,128,128]{2,1,0:T(8,128)(2,1)S(1)}, bf16[16,128,128]{2,1,0:T(8,128)(2,1)S(1)}, u32[]{:S(2)}, u32[]{:S(2)}) %collective-permute-start.1) | collective-permute-done | bytes 524320 | tf_op jit(solution)/shard_map/ppermute | solution.py:21
  31.8 5.2 %collective-permute-done = bf16[16,128,128]{2,1,0:T(8,128)(2,1)S(1)} collective-permute-done((bf16[16,128,128]{2,1,0:T(8,128)(2,1)S(1)}, bf16[16,128,128]{2,1,0:T(8,128)(2,1)S(1)}, u32[]{:S(2)}, u32[]{:S(2)}) %collective-permute-start) | collective-permute-done | bytes 524320 | tf_op jit(solution)/shard_map/ppermute | solution.py:19
  38.0 1.2 scatter_fusion
  40.1 0.9 multiply_reduce_fusion
  41.7 1.9 %fusion.7 = f32[512,512]{1,0:T(8,128)S(1)} fusion(f32[512,512]{1,0:T(8,128)S(1)} %get-tuple-element.3, f32[]{:T(128)S(6)} %mul_shard_map.3, f32[]{:T(128)} %bitcast.77), kind=kOutput, calls=%fused_computation.30 | convolution fusion | flops 1611661312 | bytes 2097160 | tf_op jit(solution)/shard_map/dot_general | solution.py:45
  43.6 2.0 %fusion.1 = f32[512,512]{1,0:T(8,128)S(1)} fusion(f32[512,512]{1,0:T(8,128)S(1)} %fusion.7, f32[]{:T(128)S(6)} %mul_shard_map.3, f32[512,512]{1,0:T(8,128)S(1)} %get-tuple-element.3, f32[]{:T(128)} %bitcast.76), kind=kOutput, calls=%fused_computation.10 | convolution fusion | flops 1613496320 | bytes 3145736 | tf_op jit(solution)/shard_map/dot_general | solution.py:48
  45.6 1.8 %fusion.21 = f32[512,512]{1,0:T(8,128)S(1)} fusion(f32[512,512]{1,0:T(8,128)S(1)} %fusion.1), kind=kOutput, calls=%fused_computation.61 | convolution fusion | flops 1610612736 | bytes 2097152 | tf_op jit(solution)/shard_map/dot_general | solution.py:45
  47.4 1.9 %fusion.3 = f32[512,512]{1,0:T(8,128)S(1)} fusion(f32[512,512]{1,0:T(8,128)S(1)} %fusion.1, f32[512,512]{1,0:T(8,128)S(1)} %fusion.21), kind=kOutput, calls=%fused_computation.12 | convolution fusion | flops 1612447744 | bytes 3145728 | tf_op jit(solution)/shard_map/dot_general | solution.py:48
  49.3 1.8 %fusion.22 = f32[512,512]{1,0:T(8,128)S(1)} fusion(f32[512,512]{1,0:T(8,128)S(1)} %fusion.3, f32[512,512]{1,0:T(8,128)S(1)} %get-tuple-element.3), kind=kOutput, calls=%fused_computation.62 | convolution fusion | flops 1610612736 | bytes 3145728 | tf_op jit(solution)/shard_map/dot_general | solution.py:52
  51.7 1.5 gather_fusion.1
  54.9 0.9 pad_maximum_fusion.2
  55.8 33.3 %all-gather.3.cloned.1.call-done = bf16[2,40,128,128]{3,2,1,0:T(8,128)(2,1)} async-done(((bf16[2,10,128,128]{3,2,1,0:T(8,128)(2,1)}), bf16[2,40,128,128]{3,2,1,0:T(8,128)(2,1)}) %all-gather.3.cloned.1.call-update) | async-done | bytes 2621456 | tf_op jit(solution)/shard_map/all_gather | solution.py:85
  89.1 4.9 %collective-permute-start.3 = (bf16[2,40,128,128]{3,2,1,0:T(8,128)(2,1)}, bf16[2,40,128,128]{3,2,1,0:T(8,128)(2,1)S(1)}, u32[]{:S(2)}, u32[]{:S(2)}) collective-permute-start(bf16[2,40,128,128]{3,2,1,0:T(8,128)(2,1)} %all-gather.3.cloned.1.call-done), channel_id=1, source_target_pairs={{4,0},{8,4},{12,8},{16,12},{20,16},{24,20},{28,24},{32,28},{36,32}... | collective-permute-start | bytes 7864328 | tf_op jit(solution)/shard_map/ppermute | solution.py:21
  95.4 7.0 %all-reduce = s32[40]{0:T(128)S(1)} all-reduce(s32[40]{0:T(128)S(1)} %bitcast_dynamic-update-slice_fusion), channel_id=2, replica_groups=mesh['slab'=64,'layer'=4] {'layer'}, use_global_device_ids=true, to_apply=%add | all-reduce | flops 40 | bytes 320 | tf_op jit(solution)/shard_map/all_gather | solution.py:86
  102.4 3.4 %collective-permute-start.5 = (s32[40]{0:T(128)S(1)}, s32[40]{0:T(128)S(1)}, u32[]{:S(2)}, u32[]{:S(2)}) collective-permute-start(s32[40]{0:T(128)S(1)} %all-reduce), channel_id=1, source_target_pairs={{4,0},{8,4},{12,8},{16,12},{20,16},{24,20},{28,24},{32,28},{36,32}... | collective-permute-start | bytes 488 | tf_op jit(solution)/shard_map/ppermute | solution.py:21
  105.9 17.7 %collective-permute-done.5 = s32[40]{0:T(128)S(1)} collective-permute-done((s32[40]{0:T(128)S(1)}, s32[40]{0:T(128)S(1)}, u32[]{:S(2)}, u32[]{:S(2)}) %collective-permute-start.5) | collective-permute-done | bytes 192 | tf_op jit(solution)/shard_map/ppermute | solution.py:21
  123.5 5.2 %collective-permute-done.4 = s32[40]{0:T(128)S(1)} collective-permute-done((s32[40]{0:T(128)S(1)}, s32[40]{0:T(128)S(1)}, u32[]{:S(2)}, u32[]{:S(2)}) %collective-permute-start.4) | collective-permute-done | bytes 192 | tf_op jit(solution)/shard_map/ppermute | solution.py:19
  128.8 6.3 %pad_maximum_fusion = bf16[2,120,128,128]{3,2,1,0:T(8,128)(2,1)} fusion(bf16[2,40,128,128]{3,2,1,0:T(8,128)(2,1)S(1)} %collective-permute-done.3, bf16[2,40,128,128]{3,2,1,0:T(8,128)(2,1)} %all-gather.3.cloned.1.call-done, bf16[2,40,128,128]{3,2,1,0:T(8,128)(2,1)} %collective-permute-done.2), kind=kLoop, calls=%fused_computation.5 | loop fusion | flops 7864320 | bytes 15728640 | tf_op jit(solution)/shard_map/concatenate | solution.py:17
  135.1 12.7 %reshape.269 = bf16[2,120,16384]{2,1,0:T(8,128)(2,1)} reshape(bf16[2,120,128,128]{3,2,1,0:T(8,128)(2,1)} %pad_maximum_fusion) | data formatting | bytes 15728640 | tf_op jit(solution)/shard_map/reshape | solution.py:94
  147.8 4.4 %convolution_bitcast_fusion = f32[2,4,16384]{2,1,0:T(4,128)S(1)} fusion(bf16[2,120,16384]{2,1,0:T(8,128)(2,1)} %reshape.269, s32[120]{0:T(128)S(1)} %pad_add_fusion, s32[4]{0:T(128)S(1)} %iota_add_fusion), kind=kOutput, calls=%fused_computation.4 | convolution fusion | flops 31457760 | bytes 8389104 | tf_op jit(solution)/shard_map/pk,gkf->gpf/dot_general | solution.py:95
  152.3 0.8 copy_bitcast_fusion.3
  (37 shorter events, 4.7 us)
Async XLA Ops:
  7.2 82.0 %all-gather.3.cloned.1.call-start = ((), (), s32[]{:S(2)}) async-start(), calls=%async_computation | async-start | bytes 3276800 | tf_op jit(solution)/shard_map/all_gather | solution.py:85
  20.9 10.9 %collective-permute-start.1 = (bf16[16,128,128]{2,1,0:T(8,128)(2,1)S(1)}, bf16[16,128,128]{2,1,0:T(8,128)(2,1)S(1)}, u32[]{:S(2)}, u32[]{:S(2)}) collective-permute-start(bf16[16,128,128]{2,1,0:T(8,128)(2,1)S(1)} %all_gather.9), channel_id=1, source_target_pairs={{4,0},{8,4},{12,8},{16,12},{20,16},{24,20},{28,24},{32,28},{36,32}... | collective-permute-start | bytes 1572872 | tf_op jit(solution)/shard_map/ppermute | solution.py:21
  25.1 11.9 %collective-permute-start = (bf16[16,128,128]{2,1,0:T(8,128)(2,1)S(1)}, bf16[16,128,128]{2,1,0:T(8,128)(2,1)S(1)}, u32[]{:S(2)}, u32[]{:S(2)}) collective-permute-start(bf16[16,128,128]{2,1,0:T(8,128)(2,1)S(1)} %all_gather.9), channel_id=1, source_target_pairs={{0,4},{4,8},{8,12},{12,16},{16,20},{20,24},{24,28},{28,32},{32,36}... | collective-permute-start | bytes 1572872 | tf_op jit(solution)/shard_map/ppermute | solution.py:19
  26.5 11.5 %copy-start.1 = (s32[10]{0:T(128)S(1)}, s32[10]{0:T(128)}, u32[]{:S(2)}) copy-start(s32[10]{0:T(128)} %constant.151) | copy-start | bytes 124
  53.2 1.1 copy-start.2
  53.6 1.1 copy-start
  53.7 40.4 %copy-start.4 = (u32[256]{0:T(256)S(1)}, u32[256]{0:T(256)}, u32[]{:S(2)}) copy-start(u32[256]{0:T(256)} %constant.170) | copy-start | bytes 3076
  53.7 41.6 %copy-start.3 = (s32[1,10]{1,0:T(1,128)S(1)}, s32[1,10]{1,0:T(1,128)}, u32[]{:S(2)}) copy-start(s32[1,10]{1,0:T(1,128)} %param.13) | copy-start | bytes 124
  89.1 39.7 %collective-permute-start.3 = (bf16[2,40,128,128]{3,2,1,0:T(8,128)(2,1)}, bf16[2,40,128,128]{3,2,1,0:T(8,128)(2,1)S(1)}, u32[]{:S(2)}, u32[]{:S(2)}) collective-permute-start(bf16[2,40,128,128]{3,2,1,0:T(8,128)(2,1)} %all-gather.3.cloned.1.call-done), channel_id=1, source_target_pairs={{4,0},{8,4},{12,8},{16,12},{20,16},{24,20},{28,24},{32,28},{36,32}... | collective-permute-start | bytes 7864328 | tf_op jit(solution)/shard_map/ppermute | solution.py:21
  94.0 34.8 %collective-permute-start.2 = (bf16[2,40,128,128]{3,2,1,0:T(8,128)(2,1)}, bf16[2,40,128,128]{3,2,1,0:T(8,128)(2,1)}, u32[]{:S(2)}, u32[]{:S(2)}) collective-permute-start(bf16[2,40,128,128]{3,2,1,0:T(8,128)(2,1)} %all-gather.3.cloned.1.call-done), channel_id=1, source_target_pairs={{0,4},{4,8},{8,12},{12,16},{16,20},{20,24},{24,28},{28,32},{32,36}... | collective-permute-start | bytes 7864328 | tf_op jit(solution)/shard_map/ppermute | solution.py:19
  102.4 21.1 %collective-permute-start.5 = (s32[40]{0:T(128)S(1)}, s32[40]{0:T(128)S(1)}, u32[]{:S(2)}, u32[]{:S(2)}) collective-permute-start(s32[40]{0:T(128)S(1)} %all-reduce), channel_id=1, source_target_pairs={{4,0},{8,4},{12,8},{16,12},{20,16},{24,20},{28,24},{32,28},{36,32}... | collective-permute-start | bytes 488 | tf_op jit(solution)/shard_map/ppermute | solution.py:21
  105.9 22.9 %collective-permute-start.4 = (s32[40]{0:T(128)S(1)}, s32[40]{0:T(128)S(1)}, u32[]{:S(2)}, u32[]{:S(2)}) collective-permute-start(s32[40]{0:T(128)S(1)} %all-reduce), channel_id=1, source_target_pairs={{0,4},{4,8},{8,12},{12,16},{16,20},{20,24},{24,28},{28,32},{32,36}... | collective-permute-start | bytes 488 | tf_op jit(solution)/shard_map/ppermute | solution.py:19
Sparse Core Ops, SparseCore 0:
  55.9 33.1 all-gather.2
where the time goes:
time: 161 us; the launch traced here: 160 us
  waiting for transfers between devices  66.8 us (41%)
  blocking collectives  20.7 us (13%)
  local copies, waits for them, and re-layouts  20.3 us (13%)
  between operations  16.3 us (10%)
  matrix products  13.9 us (9%)
  starting transfers between devices  12.6 us (8%)
  other arithmetic  9.3 us (6%)
    all_gather x1, waiting for transfers between devices, shards(): lax.all_gather(stacked, 'layer', axis=1, tiled=True)  33.3 us
    ppermute x3, waiting for transfers between devices, with_halo(): lax.ppermute(head, axis, [((i + 1) % count, i) for i in range(count)])  23 us
    all_gather x1, blocking collectives, shards(): column = lax.all_gather(hamilton_blocks, 'layer', axis=0, tiled=True)  13.7 us
    reshape x1, local copies, waits for them, and re-layouts, shards(): flat = near_parts.reshape(2, near_parts.shape[1], flat_size)  12.7 us
    ppermute x3, starting transfers between devices, with_halo(): lax.ppermute(head, axis, [((i + 1) % count, i) for i in range(count)])  12.6 us
    ppermute x3, waiting for transfers between devices, with_halo(): lax.ppermute(tail, axis, [(i, (i + 1) % count) for i in range(count)])  10.5 us
    all_gather x1, blocking collectives, shards(): lax.all_gather(requests, 'layer', axis=0, tiled=True)  7.02 us
    concatenate x3, other arithmetic, with_halo(): jnp.concatenate([lax.ppermute(tail, axis, [(i, (i + 1) % count) for i in...  6.5 us
  transfers between devices with their start and end apart: 7, of which 5 were waited for; matrix products, arithmetic and copies ran while one was open for 1% of the time, Pallas kernels for 0%

commit v1 on v0

v1 whole, which is shorter than its diff:
```python
import functools

import jax
import jax.numpy as jnp
import numpy as np
from jax import lax
from jax.experimental import pallas as pl
from jax.experimental.pallas import tpu as pltpu
from jax.sharding import PartitionSpec as P

BS = 128
NB = 4
NPS = 10
ORDER = 512
SLOTS = 4
MESH = pl.DeviceIdType.MESH
F32 = jnp.float32
BF16 = jnp.bfloat16
PAIRS = [(a, b) for a in range(NB) for b in range(a, NB)]
NO_PART = NPS


def mm(a, b):
    return jnp.dot(a, b, preferred_element_type=F32)


def eye(order, value):
    r = lax.broadcasted_iota(jnp.int32, (order, order), 0)
    c = lax.broadcasted_iota(jnp.int32, (order, order), 1)
    return jnp.where(r == c, value, 0.0)


def mean_diagonal(m):
    total = None
    for a in range(NB):
        s = slice(a * BS, (a + 1) * BS)
        r = lax.broadcasted_iota(jnp.int32, (BS, BS), 0)
        c = lax.broadcasted_iota(jnp.int32, (BS, BS), 1)
        part = jnp.where(r == c, m[s, s], 0.0)
        total = part if total is None else total + part
    return jnp.sum(total, keepdims=True) * (1.0 / ORDER)


def kernel(
    n_slab,
    hb_ref,
    ids_ref,
    w_ref,
    mu_ref,
    dens_ref,
    energy_ref,
    near,
    d_parts,
    e_parts,
    remote_ids,
    inverse,
    h_mat,
    d_sums,
    e_sums,
    d_far,
    e_far,
    d_got,
    e_got,
    local_sem,
    gather_send,
    gather_recv,
    ids_send,
    ids_recv,
    part_send,
    part_recv,
    sum_send,
    sum_recv,
):
    slab = lax.axis_index("slab")
    layer = lax.axis_index("layer")
    core = lax.rem(slab, 2)
    partner_slab = slab + 1 - 2 * core
    other_slab = lax.rem(slab - 1 + 2 * core + n_slab, n_slab)
    up_layer = lax.rem(layer + 1, 4)
    down_layer = lax.rem(layer + 3, 4)
    far_layer = lax.rem(layer + 2, 4)
    up, down = (slab, up_layer), (slab, down_layer)
    partner, other = (partner_slab, layer), (other_slab, layer)

    def remote(src, dst, send, recv, device):
        return pltpu.make_async_remote_copy(
            src_ref=src, dst_ref=dst, send_sem=send, recv_sem=recv, device_id=device, device_id_type=MESH
        )

    own_copy = pltpu.make_async_copy(hb_ref, near.at[pl.ds(layer * SLOTS, SLOTS)], local_sem)
    own_copy.start()

    barrier = pltpu.get_barrier_semaphore()
    for device in (up, down, partner, other):
        pl.semaphore_signal(barrier, inc=1, device_id=device, device_id_type=MESH)
    pl.semaphore_wait(barrier, 4)

    def piece(group, which_layer, first, count):
        return near.at[pl.ds(group * 16 + which_layer * SLOTS + first, count)]

    ids_copies = []
    for j, device in enumerate((partner, other)):
        ids_copies.append(remote(ids_ref, remote_ids.at[j], ids_send.at[j], ids_recv.at[j], device))
        ids_copies[-1].start()

    started = []

    def send(src, group, which_layer, first, count, index, device):
        c = remote(src, piece(group, which_layer, first, count), gather_send.at[index], gather_recv.at[index], device)
        c.start()
        started.append(c)

    send(hb_ref, 2, layer, 0, 4, 0, other)
    send(hb_ref, 0, layer, 0, 4, 1, up)
    send(hb_ref, 0, layer, 0, 4, 2, down)
    send(hb_ref, 1, layer, 0, 4, 3, partner)

    def wait_recv(group, which_layer, first, count, index):
        at = piece(group, which_layer, first, count)
        remote(at, at, gather_send.at[index], gather_recv.at[index], up).wait_recv()

    wait_recv(0, down_layer, 0, 4, 1)
    send(piece(0, down_layer, 0, 2), 0, down_layer, 0, 2, 4, up)
    send(piece(0, down_layer, 0, 4), 2, down_layer, 0, 4, 5, other)
    send(piece(0, down_layer, 0, 4), 1, down_layer, 0, 4, 6, partner)
    wait_recv(0, up_layer, 0, 4, 2)
    send(piece(0, up_layer, 2, 2), 0, up_layer, 2, 2, 7, down)
    send(piece(0, up_layer, 0, 4), 2, up_layer, 0, 4, 8, other)
    send(piece(0, up_layer, 0, 4), 1, up_layer, 0, 4, 9, partner)
    wait_recv(0, far_layer, 0, 2, 4)
    send(piece(0, far_layer, 0, 2), 2, far_layer, 0, 2, 10, other)
    send(piece(0, far_layer, 0, 2), 1, far_layer, 0, 2, 11, partner)
    wait_recv(0, far_layer, 2, 2, 7)
    send(piece(0, far_layer, 2, 2), 2, far_layer, 2, 2, 12, other)
    send(piece(0, far_layer, 2, 2), 1, far_layer, 2, 2, 13, partner)

    zero_block = jnp.zeros((BS, BS), BF16)
    for j in range(3):
        d_parts[j, NO_PART] = zero_block
        e_parts[j, NO_PART] = zero_block
    for c in ids_copies:
        c.wait_recv()

    def find(s, _):
        want = slab * 16 + s
        found = [NO_PART + 0 * want for _ in range(3)]
        for k in range(NPS):
            found[0] = jnp.where(ids_ref[0, k] == want, k, found[0])
            found[1] = jnp.where(remote_ids[0, 0, k] == want, k, found[1])
            found[2] = jnp.where(remote_ids[1, 0, k] == want, k, found[2])
        for j in range(3):
            inverse[j, s] = found[j]
        return 0

    lax.fori_loop(0, 16, find, 0)

    own_copy.wait()
    wait_recv(2, layer, 0, 4, 0)
    wait_recv(1, layer, 0, 4, 3)
    wait_recv(2, down_layer, 0, 4, 5)
    wait_recv(1, down_layer, 0, 4, 6)
    wait_recv(2, up_layer, 0, 4, 8)
    wait_recv(1, up_layer, 0, 4, 9)
    wait_recv(2, far_layer, 0, 2, 10)
    wait_recv(1, far_layer, 0, 2, 11)
    wait_recv(2, far_layer, 2, 2, 12)
    wait_recv(1, far_layer, 2, 2, 13)

    for k, (a, b) in enumerate(PAIRS):
        request = ids_ref[0, k]
        its_slab = request // 16
        group = jnp.where(its_slab == slab, 0, jnp.where(its_slab == partner_slab, 1, 2))
        block = near[group * 16 + request - its_slab * 16].astype(F32)
        ra, rb = pl.ds(a * BS, BS), pl.ds(b * BS, BS)
        if a == b:
            h_mat[ra, ra] = block + block.T
        else:
            h_mat[ra, rb] = block
            h_mat[rb, ra] = block.T
    h = h_mat[...]
    mu = mu_ref[0]
    norm2 = jnp.zeros((BS, BS), F32)
    for a in range(NB):
        for b in range(NB):
            block = h[a * BS : (a + 1) * BS, b * BS : (b + 1) * BS]
            if a == b:
                block = eye(BS, mu) - block
            norm2 += block * block
    norm2 = jnp.sum(norm2, keepdims=True) * (1.0 / ORDER) + 1e-06
    inv = 0.5 * lax.rsqrt(norm2)
    hb = h.astype(BF16)
    x0 = mu * inv
    s0 = (inv * inv) * mm(hb, hb) - (2.0 * x0 * inv) * h + eye(ORDER, x0 * x0 - 0.25)
    x1 = (-1.375 * inv) * h - (0.5 * x0) * s0 + (0.5 * inv) * mm(hb, s0.astype(BF16)) + eye(ORDER, 1.375 * x0)
    t1 = mean_diagonal(x1)
    b1 = x1 - eye(ORDER, t1)
    b1h = b1.astype(BF16)
    s1 = mm(b1h, b1h) + (2.0 * t1) * b1 + eye(ORDER, t1 * t1)
    u1 = mean_diagonal(s1)
    s1 = s1 - eye(ORDER, u1)
    x2 = (1.5 - 0.5 * u1) * x1 - (0.5 * t1) * s1 - 0.5 * mm(b1h, s1.astype(BF16))

    weights = [w_ref[0, k] for k in range(NPS)]
    for k, (a, b) in enumerate(PAIRS):
        block = x2[a * BS : (a + 1) * BS, b * BS : (b + 1) * BS]
        if a == b:
            block = block + eye(BS, 1.0)
        d_parts[0, k] = ((0.5 * weights[k]) * block).astype(BF16)

    part_copies = []

    def send_parts(parts, index):
        for j, device in ((2, other), (1, partner)):
            c = remote(
                parts.at[0, pl.ds(0, NPS)],
                parts.at[j, pl.ds(0, NPS)],
                part_send.at[index + j - 1],
                part_recv.at[index + j - 1],
                device,
            )
            c.start()
            part_copies.append(c)

    send_parts(d_parts, 0)

    t2 = mean_diagonal(x2)
    c2 = x2 - eye(ORDER, t2)
    c2h = c2.astype(BF16)
    c2l = (c2 - c2h.astype(F32)).astype(BF16)
    hl = (h - hb.astype(F32)).astype(BF16)
    e2 = (1.0 + t2) * h + mm(c2h, hb) + mm(c2l, hb) + mm(c2h, hl)
    for k, (a, b) in enumerate(PAIRS):
        block = e2[a * BS : (a + 1) * BS, b * BS : (b + 1) * BS]
        e_parts[0, k] = ((0.5 * weights[k]) * block).astype(BF16)
    send_parts(e_parts, 2)

    def collect(parts, which_layer, j):
        s = which_layer * SLOTS + j
        return (
            parts[0, inverse[0, s]].astype(F32)
            + parts[1, inverse[1, s]].astype(F32)
            + parts[2, inverse[2, s]].astype(F32)
        )

    sum_copies = []

    def total(parts, sums, far, got, out, base):
        part_copies[base // 3].wait_recv()
        part_copies[base // 3 + 1].wait_recv()

        def move(src, dst, index, device):
            c = remote(src, dst, sum_send.at[base + index], sum_recv.at[base + index], device)
            c.start()
            sum_copies.append(c)
            return c

        for j in range(2):
            sums[2, j] = collect(parts, far_layer, j).astype(BF16)
        f_up = move(sums.at[2, pl.ds(0, 2)], far.at[0], 0, up)
        for j in range(2, 4):
            sums[2, j] = collect(parts, far_layer, j).astype(BF16)
        f_down = move(sums.at[2, pl.ds(2, 2)], far.at[1], 1, down)
        for j in range(2, 4):
            sums[0, j] = collect(parts, up_layer, j).astype(BF16)
        h_up = move(sums.at[0, pl.ds(2, 2)], got.at[0, pl.ds(2, 2)], 2, up)
        for j in range(2):
            sums[1, j] = collect(parts, down_layer, j).astype(BF16)
        h_down = move(sums.at[1, pl.ds(0, 2)], got.at[1, pl.ds(0, 2)], 3, down)
        f_up.wait_recv()
        for j in range(2):
            sums[0, j] = (collect(parts, up_layer, j) + far[0, j].astype(F32)).astype(BF16)
        a_up = move(sums.at[0, pl.ds(0, 2)], got.at[0, pl.ds(0, 2)], 4, up)
        f_down.wait_recv()
        for j in range(2, 4):
            sums[1, j] = (collect(parts, down_layer, j) + far[1, j - 2].astype(F32)).astype(BF16)
        a_down = move(sums.at[1, pl.ds(2, 2)], got.at[1, pl.ds(2, 2)], 5, down)
        for j in range(4):
            out[j] = collect(parts, layer, j)
        return h_up, h_down, a_up, a_down

    def finish(waits, got, out):
        for c in waits:
            c.wait_recv()
        for j in range(4):
            out[j] = out[j] + (got[0, j].astype(F32) + got[1, j].astype(F32))

    d_waits = total(d_parts, d_sums, d_far, d_got, dens_ref, 0)
    e_waits = total(e_parts, e_sums, e_far, e_got, energy_ref, 6)
    finish(d_waits, d_got, dens_ref)
    finish(e_waits, e_got, energy_ref)

    for c in ids_copies + started + part_copies + sum_copies:
        c.wait_send()


def solution(mesh):
    n_slab = mesh.shape["slab"]

    def step(hamilton_blocks, pair_ids, weights, potential):
        smem = pl.BlockSpec(memory_space=pltpu.SMEM)
        vmem = pl.BlockSpec(memory_space=pltpu.VMEM)
        dma = pltpu.SemaphoreType.DMA
        out = jax.ShapeDtypeStruct((SLOTS, BS, BS), F32)
        return pl.pallas_call(
            functools.partial(kernel, n_slab),
            out_shape=(out, out),
            in_specs=[pl.BlockSpec(memory_space=pl.ANY), smem, smem, smem],
            out_specs=(vmem, vmem),
            scratch_shapes=[
                pltpu.VMEM((48, BS, BS), BF16),
                pltpu.VMEM((3, NPS + 1, BS, BS), BF16),
                pltpu.VMEM((3, NPS + 1, BS, BS), BF16),
                pltpu.SMEM((2, 1, NPS), jnp.int32),
                pltpu.SMEM((3, 16), jnp.int32),
                pltpu.VMEM((ORDER, ORDER), F32),
                pltpu.VMEM((3, SLOTS, BS, BS), BF16),
                pltpu.VMEM((3, SLOTS, BS, BS), BF16),
                pltpu.VMEM((2, 2, BS, BS), BF16),
                pltpu.VMEM((2, 2, BS, BS), BF16),
                pltpu.VMEM((2, SLOTS, BS, BS), BF16),
                pltpu.VMEM((2, SLOTS, BS, BS), BF16),
                dma,
                dma((14,)),
                dma((14,)),
                dma((2,)),
                dma((2,)),
                dma((4,)),
                dma((4,)),
                dma((12,)),
                dma((12,)),
            ],
            compiler_params=pltpu.CompilerParams(
                collective_id=0, has_side_effects=True, vmem_limit_bytes=48 * 1024 * 1024
            ),
        )(hamilton_blocks, pair_ids, weights, potential)

    return jax.shard_map(
        step,
        mesh=mesh,
        in_specs=(P(("slab", "layer"), None, None), P(("slab", "layer"), None), P(("slab", "layer"), None), P()),
        out_specs=(P(("slab", "layer"), None, None), P(("slab", "layer"), None, None)),
        check_vma=False,
    )
```

time: 161 us -> 48.1 us (0.30)
  waiting for transfers between devices: 66.8 us -> 0 us
  Pallas kernels: 0 us -> 44.1 us
  blocking collectives: 20.7 us -> 0 us
  local copies, waits for them, and re-layouts: 20.3 us -> 2.31 us
  between operations: 16.3 us -> 1.34 us
  matrix products: 13.9 us -> 0 us
  starting transfers between devices: 12.6 us -> 0 us
  other arithmetic: 9.3 us -> 0 us
    pallas_call x0 -> x1, Pallas kernels: none -> 44.1 us  [step(): pl.pallas_call(functools.partial(kernel, n_slab), out_shape=(out, out), i...]
    ppermute x6 -> x0, waiting for transfers between devices: 33.4 us -> none  [the longest x3 23 us: with_halo(): lax.ppermute(head, axis, [((i + 1) % count, i) for i in range(count)])]
    all_gather x1 -> x0, waiting for transfers between devices: 33.3 us -> none  [shards(): lax.all_gather(stacked, 'layer', axis=1, tiled=True)]
    all_gather x2 -> x0, blocking collectives: 20.7 us -> none  [the longest x1 13.7 us: shards(): column = lax.all_gather(hamilton_blocks, 'layer', axis=0, tiled=True)]
    reshape x6 -> x0, local copies, waits for them, and re-layouts: 14 us -> none  [the longest x1 12.7 us: shards(): flat = near_parts.reshape(2, near_parts.shape[1], flat_size)]
    dot_general x6 -> x0, matrix products: 13.9 us -> none  [the longest x1 4.44 us: shards(): jnp.einsum('pk,gkf->gpf', match_table, flat, preferred_element_type=jnp.f...]
    ppermute x6 -> x0, starting transfers between devices: 12.6 us -> none  [the longest x3 12.6 us: with_halo(): lax.ppermute(head, axis, [((i + 1) % count, i) for i in range(count)])]
    concatenate x3 -> x0, other arithmetic: 6.5 us -> none  [with_halo(): jnp.concatenate([lax.ppermute(tail, axis, [(i, (i + 1) % count) for i in...]
  transfers between devices with their start and end apart: 7 -> 0, of which waited for: 5 -> 0; matrix products, arithmetic and copies ran while one was open for 1% -> 0% of each run, Pallas kernels for 0% -> 0%
where the time goes in v1:
time: 48.1 us; the launch traced here: 47.7 us
  Pallas kernels  44.1 us (92%)
  local copies, waits for them, and re-layouts  2.31 us (5%)
  between operations  1.34 us (3%)
    pallas_call x1, Pallas kernels, step(): pl.pallas_call(functools.partial(kernel, n_slab), out_shape=(out, out), i...  44.1 us
    unnamed x8, local copies, waits for them, and re-layouts  2.31 us

profile of v1, /device:TPU:2, one launch (start us, length us, event | category | flops | bytes accessed | tf_op | source)
XLA Modules:
  0.0 47.7 jit_solution(13908881575831985928)
XLA Ops:
  0.6 0.0 copy-start.2
  0.6 0.0 copy-start.1
  1.3 0.0 copy-done.2
  1.3 0.0 copy-done.1
  1.3 0.0 copy-start
  1.3 0.9 %copy-done = bf16[4,128,128]{2,1,0:T(8,128)(2,1)S(1)} copy-done((bf16[4,128,128]{2,1,0:T(8,128)(2,1)S(1)}, bf16[4,128,128]{2,1,0:T(8,128)(2,1)}, u32[]{:S(2)}) %copy-start) | copy-done | bytes 131096
  2.2 44.1 %shard_map.59 = (f32[4,128,128]{2,1,0:T(8,128)S(1)}, f32[4,128,128]{2,1,0:T(8,128)S(1)}) custom-call(bf16[4,128,128]{2,1,0:T(8,128)(2,1)S(1)} %copy-done, s32[1,10]{1,0:T(1,128)S(1)} %copy-done.1, f32[1,10]{1,0:T(1,128)S(1)} %copy-done.2, f32[1]{0:T(128)S(6)} %copy.8.mu_ref), custom_call_target="tpu_custom_call" | custom-call | tf_op jit(solution)/shard_map/pallas_call | solution.py:304
  46.3 0.7 %copy.9 = f32[4,128,128]{2,1,0:T(8,128)} copy(f32[4,128,128]{2,1,0:T(8,128)S(1)} %get-tuple-element.4) | data formatting | bytes 524288
  47.0 0.7 %copy.10 = f32[4,128,128]{2,1,0:T(8,128)} copy(f32[4,128,128]{2,1,0:T(8,128)S(1)} %get-tuple-element.5) | data formatting | bytes 524288
Async XLA Ops:
  0.6 0.7 %copy-start.2 = (f32[1,10]{1,0:T(1,128)S(1)}, f32[1,10]{1,0:T(1,128)}, u32[]{:S(2)}) copy-start(f32[1,10]{1,0:T(1,128)} %w_ref.1) | copy-start | bytes 124
  0.6 0.7 %copy-start.1 = (s32[1,10]{1,0:T(1,128)S(1)}, s32[1,10]{1,0:T(1,128)}, u32[]{:S(2)}) copy-start(s32[1,10]{1,0:T(1,128)} %ids_ref.1) | copy-start | bytes 124
  1.3 0.9 %copy-start = (bf16[4,128,128]{2,1,0:T(8,128)(2,1)S(1)}, bf16[4,128,128]{2,1,0:T(8,128)(2,1)}, u32[]{:S(2)}) copy-start(bf16[4,128,128]{2,1,0:T(8,128)(2,1)} %hb_ref.1) | copy-start | bytes 393220

commit v2 on v1

v2 whole, which is shorter than its diff:
```python
import functools

import jax
import jax.numpy as jnp
import numpy as np
from jax import lax
from jax.experimental import pallas as pl
from jax.experimental.pallas import tpu as pltpu
from jax.sharding import PartitionSpec as P

BS = 128
NB = 4
NPS = 10
ORDER = 512
SLOTS = 4
HALF = BS // 2
MESH = pl.DeviceIdType.MESH
F32 = jnp.float32
BF16 = jnp.bfloat16
PAIRS = [(a, b) for a in range(NB) for b in range(a, NB)]
NO_PART = NPS


def mm(a, b):
    return jnp.dot(a, b, preferred_element_type=F32)


def eye(order, value):
    r = lax.broadcasted_iota(jnp.int32, (order, order), 0)
    c = lax.broadcasted_iota(jnp.int32, (order, order), 1)
    return jnp.where(r == c, value, 0.0)


def mean_diagonal(m):
    total = None
    for a in range(NB):
        s = slice(a * BS, (a + 1) * BS)
        r = lax.broadcasted_iota(jnp.int32, (BS, BS), 0)
        c = lax.broadcasted_iota(jnp.int32, (BS, BS), 1)
        part = jnp.where(r == c, m[s, s], 0.0)
        total = part if total is None else total + part
    return jnp.sum(total, keepdims=True) * (1.0 / ORDER)


def kernel(
    n_slab,
    hb_ref,
    ids_hbm,
    w_hbm,
    mu_ref,
    dens_ref,
    energy_ref,
    near,
    parts0,
    parts1,
    parts2,
    parts3,
    ids_ref,
    w_ref,
    remote_ids,
    inverse,
    h_mat,
    sums,
    far,
    got,
    local_sem,
    small_sem,
    gather_send,
    gather_recv,
    ids_send,
    ids_recv,
    part_send,
    part_recv,
    sum_send,
    sum_recv,
):
    slab = lax.axis_index("slab")
    layer = lax.axis_index("layer")
    core = lax.rem(slab, 2)
    partner_slab = slab + 1 - 2 * core
    other_slab = lax.rem(slab - 1 + 2 * core + n_slab, n_slab)
    up_layer = lax.rem(layer + 1, 4)
    down_layer = lax.rem(layer + 3, 4)
    far_layer = lax.rem(layer + 2, 4)
    up, down = (slab, up_layer), (slab, down_layer)
    partner, other = (partner_slab, layer), (other_slab, layer)
    parts = (parts0, parts1, parts2, parts3)

    def remote(src, dst, send, recv, device):
        return pltpu.make_async_remote_copy(
            src_ref=src, dst_ref=dst, send_sem=send, recv_sem=recv, device_id=device, device_id_type=MESH
        )

    barrier = pltpu.get_barrier_semaphore()
    for device in (other, up, down, partner):
        pl.semaphore_signal(barrier, inc=1, device_id=device, device_id_type=MESH)
    locals_ = [pltpu.make_async_copy(hb_ref, near.at[pl.ds(layer * SLOTS, SLOTS)], local_sem)]
    for i, (src, dst) in enumerate(((ids_hbm, ids_ref), (w_hbm, w_ref))):
        locals_.append(pltpu.make_async_copy(src, dst, small_sem.at[i]))
    for c in locals_:
        c.start()
    zero_block = jnp.zeros((HALF, BS), BF16)
    for part in parts:
        for j in range(3):
            part[j, NO_PART] = zero_block
    pl.semaphore_wait(barrier, 4)

    def piece(group, which_layer, first, count):
        return near.at[pl.ds(group * 16 + which_layer * SLOTS + first, count)]

    started = []

    def send(src, group, which_layer, first, count, index, device):
        c = remote(src, piece(group, which_layer, first, count), gather_send.at[index], gather_recv.at[index], device)
        c.start()
        started.append(c)

    def wait_recv(group, which_layer, first, count, index):
        at = piece(group, which_layer, first, count)
        remote(at, at, gather_send.at[index], gather_recv.at[index], up).wait_recv()

    send(hb_ref.at[pl.ds(0, 2)], 0, layer, 0, 2, 0, up)
    send(hb_ref.at[pl.ds(2, 2)], 0, layer, 2, 2, 1, down)
    send(hb_ref, 2, layer, 0, 4, 2, other)
    send(hb_ref.at[pl.ds(2, 2)], 0, layer, 2, 2, 3, up)
    send(hb_ref.at[pl.ds(0, 2)], 0, layer, 0, 2, 4, down)
    send(hb_ref, 1, layer, 0, 4, 5, partner)
    ids_copies = []
    for j, device in enumerate((partner, other)):
        ids_copies.append(remote(ids_hbm, remote_ids.at[j], ids_send.at[j], ids_recv.at[j], device))
        ids_copies[-1].start()

    relays = (
        (down_layer, 0, 0, 6, up),
        (up_layer, 2, 1, 7, down),
        (down_layer, 2, 3, None, None),
        (up_layer, 0, 4, None, None),
        (far_layer, 0, 6, None, None),
        (far_layer, 2, 7, None, None),
    )
    for i, (which, first, index, onward, device) in enumerate(relays):
        wait_recv(0, which, first, 2, index)
        if onward is not None:
            send(piece(0, which, first, 2), 0, which, first, 2, onward, device)
        send(piece(0, which, first, 2), 2, which, first, 2, 8 + i, other)
        send(piece(0, which, first, 2), 1, which, first, 2, 14 + i, partner)

    for c in locals_:
        c.wait()
    for c in ids_copies:
        c.wait_recv()

    def find(s, _):
        want = slab * 16 + s
        found = [NO_PART + 0 * want for _ in range(3)]
        for k in range(NPS):
            found[0] = jnp.where(ids_ref[0, k] == want, k, found[0])
            found[1] = jnp.where(remote_ids[0, 0, k] == want, k, found[1])
            found[2] = jnp.where(remote_ids[1, 0, k] == want, k, found[2])
        for j in range(3):
            inverse[j, s] = found[j]
        return 0

    lax.fori_loop(0, 16, find, 0)

    wait_recv(1, layer, 0, 4, 5)
    wait_recv(2, layer, 0, 4, 2)
    for i, (which, first, _, _, _) in enumerate(relays):
        wait_recv(1, which, first, 2, 14 + i)
        wait_recv(2, which, first, 2, 8 + i)

    for k, (a, b) in enumerate(PAIRS):
        request = ids_ref[0, k]
        its_slab = request // 16
        group = jnp.where(its_slab == slab, 0, jnp.where(its_slab == partner_slab, 1, 2))
        block = near[group * 16 + request - its_slab * 16].astype(F32)
        ra, rb = pl.ds(a * BS, BS), pl.ds(b * BS, BS)
        if a == b:
            h_mat[ra, ra] = block + block.T
        else:
            h_mat[ra, rb] = block
            h_mat[rb, ra] = block.T
    h = h_mat[...]
    mu = mu_ref[0]
    norm2 = jnp.zeros((BS, BS), F32)
    for a in range(NB):
        for b in range(NB):
            block = h[a * BS : (a + 1) * BS, b * BS : (b + 1) * BS]
            if a == b:
                block = eye(BS, mu) - block
            norm2 += block * block
    norm2 = jnp.sum(norm2, keepdims=True) * (1.0 / ORDER) + 1e-06
    inv = 0.5 * lax.rsqrt(norm2)
    hb = h.astype(BF16)
    x0 = mu * inv
    s0 = (inv * inv) * mm(hb, hb) - (2.0 * x0 * inv) * h + eye(ORDER, x0 * x0 - 0.25)
    x1 = (-1.375 * inv) * h - (0.5 * x0) * s0 + (0.5 * inv) * mm(hb, s0.astype(BF16)) + eye(ORDER, 1.375 * x0)
    t1 = mean_diagonal(x1)
    b1 = x1 - eye(ORDER, t1)
    b1h = b1.astype(BF16)
    s1 = mm(b1h, b1h) + (2.0 * t1) * b1 + eye(ORDER, t1 * t1)
    u1 = mean_diagonal(s1)
    s1 = s1 - eye(ORDER, u1)
    x2 = (1.5 - 0.5 * u1) * x1 - (0.5 * t1) * s1 - 0.5 * mm(b1h, s1.astype(BF16))

    weights = [0.5 * w_ref[0, k] for k in range(NPS)]
    part_copies = []

    def store_parts(matrix, chunk, half, identity):
        for k, (a, b) in enumerate(PAIRS):
            first = a * BS + half * HALF
            block = matrix[first : first + HALF, b * BS : (b + 1) * BS]
            if identity and a == b:
                r = lax.broadcasted_iota(jnp.int32, (HALF, BS), 0) + half * HALF
                c = lax.broadcasted_iota(jnp.int32, (HALF, BS), 1)
                block = block + jnp.where(r == c, 1.0, 0.0)
            parts[chunk][0, k] = (weights[k] * block).astype(BF16)
        for j, device in ((2, other), (1, partner)):
            c = remote(
                parts[chunk].at[0, pl.ds(0, NPS)],
                parts[chunk].at[j, pl.ds(0, NPS)],
                part_send.at[2 * chunk + j - 1],
                part_recv.at[2 * chunk + j - 1],
                device,
            )
            c.start()
            part_copies.append(c)

    store_parts(x2, 0, 0, True)
    store_parts(x2, 1, 1, True)

    t2 = mean_diagonal(x2)
    c2 = x2 - eye(ORDER, t2)
    c2h = c2.astype(BF16)
    c2l = (c2 - c2h.astype(F32)).astype(BF16)
    hl = (h - hb.astype(F32)).astype(BF16)
    e2 = (1.0 + t2) * h + mm(c2h, hb) + mm(c2l, hb) + mm(c2h, hl)
    store_parts(e2, 2, 0, False)
    store_parts(e2, 3, 1, False)

    sum_copies = []
    outs = (dens_ref, energy_ref)

    def collect(chunk, which_layer, j):
        s = which_layer * SLOTS + j
        part = parts[chunk]
        return (
            part[0, inverse[0, s]].astype(F32)
            + part[1, inverse[1, s]].astype(F32)
            + part[2, inverse[2, s]].astype(F32)
        )

    def move(src, dst, index, device):
        c = remote(src, dst, sum_send.at[index], sum_recv.at[index], device)
        c.start()
        sum_copies.append(c)
        return c

    def first_hop(chunk):
        part_copies[2 * chunk].wait_recv()
        part_copies[2 * chunk + 1].wait_recv()
        for j in range(4):
            sums[chunk, 2, j] = collect(chunk, far_layer, j).astype(BF16)
        to_up = move(sums.at[chunk, 2, pl.ds(0, 2)], far.at[chunk, 0], 4 * chunk, up)
        to_down = move(sums.at[chunk, 2, pl.ds(2, 2)], far.at[chunk, 1], 4 * chunk + 1, down)
        for j in range(2):
            sums[chunk, 0, 2 + j] = collect(chunk, up_layer, 2 + j).astype(BF16)
            sums[chunk, 1, j] = collect(chunk, down_layer, j).astype(BF16)
        return to_up, to_down

    def second_hop(chunk, arrivals):
        arrivals[0].wait_recv()
        for j in range(2):
            sums[chunk, 0, j] = (collect(chunk, up_layer, j) + far[chunk, 0, j].astype(F32)).astype(BF16)
        to_up = move(sums.at[chunk, 0], got.at[chunk, 0], 4 * chunk + 2, up)
        arrivals[1].wait_recv()
        for j in range(2):
            sums[chunk, 1, 2 + j] = (collect(chunk, down_layer, 2 + j) + far[chunk, 1, j].astype(F32)).astype(BF16)
        to_down = move(sums.at[chunk, 1], got.at[chunk, 1], 4 * chunk + 3, down)
        return to_up, to_down

    def finish(chunk, arrivals):
        for c in arrivals:
            c.wait_recv()
        rows = pl.ds((chunk % 2) * HALF, HALF)
        for j in range(4):
            outs[chunk // 2][j, rows] = collect(chunk, layer, j) + (
                got[chunk, 0, j].astype(F32) + got[chunk, 1, j].astype(F32)
            )

    ready = {0: first_hop(0)}
    done = {}
    for chunk in range(1, 4):
        ready[chunk] = first_hop(chunk)
        done[chunk - 1] = second_hop(chunk - 1, ready[chunk - 1])
    done[3] = second_hop(3, ready[3])
    for chunk in range(4):
        finish(chunk, done[chunk])

    for c in ids_copies + started + part_copies + sum_copies:
        c.wait_send()


def write_out(dens_ref, energy_ref, dens_out, energy_out, sems):
    copies = [
        pltpu.make_async_copy(dens_ref, dens_out, sems.at[0]),
        pltpu.make_async_copy(energy_ref, energy_out, sems.at[1]),
    ]
    for c in copies:
        c.start()
    for c in copies:
        c.wait()


def solution(mesh):
    n_slab = mesh.shape["slab"]

    def step(hamilton_blocks, pair_ids, weights, potential):
        hbm = pl.BlockSpec(memory_space=pltpu.HBM)
        vmem = pl.BlockSpec(memory_space=pltpu.VMEM)
        dma = pltpu.SemaphoreType.DMA
        out = jax.ShapeDtypeStruct((SLOTS, BS, BS), F32)
        sums = pl.pallas_call(
            functools.partial(kernel, n_slab),
            out_shape=(pltpu.VMEM(out.shape, F32), pltpu.VMEM(out.shape, F32)),
            in_specs=[hbm, hbm, hbm, pl.BlockSpec(memory_space=pltpu.SMEM)],
            out_specs=(vmem, vmem),
            scratch_shapes=[
                pltpu.VMEM((48, BS, BS), BF16),
                *[pltpu.VMEM((3, NPS + 1, HALF, BS), BF16)] * 4,
                pltpu.SMEM((1, NPS), jnp.int32),
                pltpu.SMEM((1, NPS), F32),
                pltpu.SMEM((2, 1, NPS), jnp.int32),
                pltpu.SMEM((3, 16), jnp.int32),
                pltpu.VMEM((ORDER, ORDER), F32),
                pltpu.VMEM((4, 3, SLOTS, HALF, BS), BF16),
                pltpu.VMEM((4, 2, 2, HALF, BS), BF16),
                pltpu.VMEM((4, 2, SLOTS, HALF, BS), BF16),
                dma,
                dma((2,)),
                dma((20,)),
                dma((20,)),
                dma((2,)),
                dma((2,)),
                dma((8,)),
                dma((8,)),
                dma((16,)),
                dma((16,)),
            ],
            compiler_params=pltpu.CompilerParams(
                collective_id=0, has_side_effects=True, vmem_limit_bytes=48 * 1024 * 1024
            ),
        )(*[pltpu.with_memory_space_constraint(x, pltpu.HBM) for x in (hamilton_blocks, pair_ids, weights)], potential)
        return pl.pallas_call(
            write_out,
            out_shape=(pltpu.HBM(out.shape, F32), pltpu.HBM(out.shape, F32)),
            in_specs=[vmem, vmem],
            out_specs=(hbm, hbm),
            scratch_shapes=[dma((2,))],
        )(*[pltpu.with_memory_space_constraint(x, pltpu.VMEM) for x in sums])

    return jax.shard_map(
        step,
        mesh=mesh,
        in_specs=(P(("slab", "layer"), None, None), P(("slab", "layer"), None), P(("slab", "layer"), None), P()),
        out_specs=(P(("slab", "layer"), None, None), P(("slab", "layer"), None, None)),
        check_vma=False,
    )
```

time: 48.1 us -> 44 us (0.915)
  local copies, waits for them, and re-layouts: 2.31 us -> 0 us
  Pallas kernels: 44.1 us -> 42.4 us
    unnamed x8 -> x0, local copies, waits for them, and re-layouts: 2.31 us -> none
    pallas_call x1 -> x2, Pallas kernels: 44.1 us -> 42.4 us  [the longest x1 41.6 us: step(): pl.pallas_call(functools.partial(kernel, n_slab), out_shape=(pltpu.VMEM(o...]
where the time goes in v2:
time: 44 us; the launch traced here: 43.7 us
  Pallas kernels  42.4 us (96%)
  between operations  1.28 us (3%)
    pallas_call x1, Pallas kernels, step(): pl.pallas_call(functools.partial(kernel, n_slab), out_shape=(pltpu.VMEM(o...  41.6 us

profile of v2, /device:TPU:2, one launch (start us, length us, event | category | flops | bytes accessed | tf_op | source)
XLA Modules:
  0.0 43.7 jit_solution(8845009939305997511)
XLA Ops:
  1.3 41.6 %shard_map.59 = (f32[4,128,128]{2,1,0:T(8,128)S(1)}, f32[4,128,128]{2,1,0:T(8,128)S(1)}) custom-call(bf16[4,128,128]{2,1,0:T(8,128)(2,1)} %hb_ref.1, s32[1,10]{1,0:T(1,128)} %ids_hbm.1, f32[1,10]{1,0:T(1,128)} %w_hbm.1, f32[1]{0:T(128)S(6)} %copy.6.mu_ref), custom_call_target="tpu_custom_call" | custom-call | tf_op jit(solution)/shard_map/pallas_call | solution.py:323
  42.9 0.8 %shard_map.60 = (f32[4,128,128]{2,1,0:T(8,128)}, f32[4,128,128]{2,1,0:T(8,128)}) custom-call(f32[4,128,128]{2,1,0:T(8,128)S(1)} %get-tuple-element.4.dens_ref, f32[4,128,128]{2,1,0:T(8,128)S(1)} %get-tuple-element.5.energy_ref), custom_call_target="tpu_custom_call" | custom-call | tf_op jit(solution)/shard_map/pallas_call | solution.py:354

commit v3 on v2

--- a/solution.py
+++ b/solution.py
@@ -13,7 +13,9 @@
 NPS = 10
 ORDER = 512
 SLOTS = 4
-HALF = BS // 2
+ROWS = 32
+CHUNKS = tuple((energy, row, ROWS) for energy in range(2) for row in range(0, BS, ROWS))
+N_CHUNK = len(CHUNKS)
 MESH = pl.DeviceIdType.MESH
 F32 = jnp.float32
 BF16 = jnp.bfloat16
@@ -42,38 +44,11 @@
     return jnp.sum(total, keepdims=True) * (1.0 / ORDER)
 
 
-def kernel(
-    n_slab,
-    hb_ref,
-    ids_hbm,
-    w_hbm,
-    mu_ref,
-    dens_ref,
-    energy_ref,
-    near,
-    parts0,
-    parts1,
-    parts2,
-    parts3,
-    ids_ref,
-    w_ref,
-    remote_ids,
-    inverse,
-    h_mat,
-    sums,
-    far,
-    got,
-    local_sem,
-    small_sem,
-    gather_send,
-    gather_recv,
-    ids_send,
-    ids_recv,
-    part_send,
-    part_recv,
-    sum_send,
-    sum_recv,
-):
+def kernel(n_slab, hb_ref, ids_hbm, w_hbm, mu_ref, dens_ref, energy_ref, near, *rest):
+    parts, sums, got = (rest[i * N_CHUNK : (i + 1) * N_CHUNK] for i in range(3))
+    ids_ref, w_ref, remote_ids, inverse, h_mat, local_sem, small_sem = rest[3 * N_CHUNK : 3 * N_CHUNK + 7]
+    gather_send, gather_recv, ids_send, ids_recv, part_send, part_recv, sum_send, sum_recv = rest[3 * N_CHUNK + 7 :]
+    outs = (dens_ref, energy_ref)
     slab = lax.axis_index("slab")
     layer = lax.axis_index("layer")
     core = lax.rem(slab, 2)
@@ -83,8 +58,7 @@
     down_layer = lax.rem(layer + 3, 4)
     far_layer = lax.rem(layer + 2, 4)
     up, down = (slab, up_layer), (slab, down_layer)
-    partner, other = (partner_slab, layer), (other_slab, layer)
-    parts = (parts0, parts1, parts2, parts3)
+    partner, other, across = (partner_slab, layer), (other_slab, layer), (slab, far_layer)
 
     def remote(src, dst, send, recv, device):
         return pltpu.make_async_remote_copy(
@@ -92,18 +66,17 @@
         )
 
     barrier = pltpu.get_barrier_semaphore()
-    for device in (other, up, down, partner):
+    for device in (other, up, down, partner, across):
         pl.semaphore_signal(barrier, inc=1, device_id=device, device_id_type=MESH)
     locals_ = [pltpu.make_async_copy(hb_ref, near.at[pl.ds(layer * SLOTS, SLOTS)], local_sem)]
     for i, (src, dst) in enumerate(((ids_hbm, ids_ref), (w_hbm, w_ref))):
         locals_.append(pltpu.make_async_copy(src, dst, small_sem.at[i]))
     for c in locals_:
         c.start()
-    zero_block = jnp.zeros((HALF, BS), BF16)
-    for part in parts:
+    for (_, _, rows), part in zip(CHUNKS, parts):
         for j in range(3):
-            part[j, NO_PART] = zero_block
-    pl.semaphore_wait(barrier, 4)
+            part[j, NO_PART] = jnp.zeros((rows, BS), BF16)
+    pl.semaphore_wait(barrier, 5)
 
     def piece(group, which_layer, first, count):
         return near.at[pl.ds(group * 16 + which_layer * SLOTS + first, count)]
@@ -125,23 +98,23 @@
     send(hb_ref.at[pl.ds(2, 2)], 0, layer, 2, 2, 3, up)
     send(hb_ref.at[pl.ds(0, 2)], 0, layer, 0, 2, 4, down)
     send(hb_ref, 1, layer, 0, 4, 5, partner)
+    send(hb_ref.at[pl.ds(0, 2)], 0, layer, 0, 2, 6, across)
+    send(hb_ref.at[pl.ds(2, 2)], 0, layer, 2, 2, 7, across)
     ids_copies = []
     for j, device in enumerate((partner, other)):
         ids_copies.append(remote(ids_hbm, remote_ids.at[j], ids_send.at[j], ids_recv.at[j], device))
         ids_copies[-1].start()
 
     relays = (
-        (down_layer, 0, 0, 6, up),
-        (up_layer, 2, 1, 7, down),
-        (down_layer, 2, 3, None, None),
-        (up_layer, 0, 4, None, None),
-        (far_layer, 0, 6, None, None),
-        (far_layer, 2, 7, None, None),
+        (down_layer, 0, 0),
+        (up_layer, 2, 1),
+        (down_layer, 2, 3),
+        (up_layer, 0, 4),
+        (far_layer, 0, 6),
+        (far_layer, 2, 7),
     )
-    for i, (which, first, index, onward, device) in enumerate(relays):
+    for i, (which, first, index) in enumerate(relays):
         wait_recv(0, which, first, 2, index)
-        if onward is not None:
-            send(piece(0, which, first, 2), 0, which, first, 2, onward, device)
         send(piece(0, which, first, 2), 2, which, first, 2, 8 + i, other)
         send(piece(0, which, first, 2), 1, which, first, 2, 14 + i, partner)
 
@@ -165,7 +138,7 @@
 
     wait_recv(1, layer, 0, 4, 5)
     wait_recv(2, layer, 0, 4, 2)
-    for i, (which, first, _, _, _) in enumerate(relays):
+    for i, (which, first, _) in enumerate(relays):
         wait_recv(1, which, first, 2, 14 + i)
         wait_recv(2, which, first, 2, 8 + i)
 
@@ -206,13 +179,14 @@
     weights = [0.5 * w_ref[0, k] for k in range(NPS)]
     part_copies = []
 
-    def store_parts(matrix, chunk, half, identity):
+    def store_parts(matrix, chunk):
+        energy, row, rows = CHUNKS[chunk]
         for k, (a, b) in enumerate(PAIRS):
-            first = a * BS + half * HALF
-            block = matrix[first : first + HALF, b * BS : (b + 1) * BS]
-            if identity and a == b:
-                r = lax.broadcasted_iota(jnp.int32, (HALF, BS), 0) + half * HALF
-                c = lax.broadcasted_iota(jnp.int32, (HALF, BS), 1)
+            first = a * BS + row
+            block = matrix[first : first + rows, b * BS : (b + 1) * BS]
+            if not energy and a == b:
+                r = lax.broadcasted_iota(jnp.int32, (rows, BS), 0) + row
+                c = lax.broadcasted_iota(jnp.int32, (rows, BS), 1)
                 block = block + jnp.where(r == c, 1.0, 0.0)
             parts[chunk][0, k] = (weights[k] * block).astype(BF16)
         for j, device in ((2, other), (1, partner)):
@@ -226,8 +200,9 @@
             c.start()
             part_copies.append(c)
 
-    store_parts(x2, 0, 0, True)
-    store_parts(x2, 1, 1, True)
+    for chunk in range(N_CHUNK):
+        if not CHUNKS[chunk][0]:
+            store_parts(x2, chunk)
 
     t2 = mean_diagonal(x2)
     c2 = x2 - eye(ORDER, t2)
@@ -235,11 +210,11 @@
     c2l = (c2 - c2h.astype(F32)).astype(BF16)
     hl = (h - hb.astype(F32)).astype(BF16)
     e2 = (1.0 + t2) * h + mm(c2h, hb) + mm(c2l, hb) + mm(c2h, hl)
-    store_parts(e2, 2, 0, False)
-    store_parts(e2, 3, 1, False)
+    for chunk in range(N_CHUNK):
+        if CHUNKS[chunk][0]:
+            store_parts(e2, chunk)
 
     sum_copies = []
-    outs = (dens_ref, energy_ref)
 
     def collect(chunk, which_layer, j):
         s = which_layer * SLOTS + j
@@ -250,52 +225,25 @@
             + part[2, inverse[2, s]].astype(F32)
         )
 
-    def move(src, dst, index, device):
-        c = remote(src, dst, sum_send.at[index], sum_recv.at[index], device)
-        c.start()
-        sum_copies.append(c)
-        return c
-
-    def first_hop(chunk):
+    for chunk in range(N_CHUNK):
         part_copies[2 * chunk].wait_recv()
         part_copies[2 * chunk + 1].wait_recv()
-        for j in range(4):
-            sums[chunk, 2, j] = collect(chunk, far_layer, j).astype(BF16)
-        to_up = move(sums.at[chunk, 2, pl.ds(0, 2)], far.at[chunk, 0], 4 * chunk, up)
-        to_down = move(sums.at[chunk, 2, pl.ds(2, 2)], far.at[chunk, 1], 4 * chunk + 1, down)
-        for j in range(2):
-            sums[chunk, 0, 2 + j] = collect(chunk, up_layer, 2 + j).astype(BF16)
-            sums[chunk, 1, j] = collect(chunk, down_layer, j).astype(BF16)
-        return to_up, to_down
-
-    def second_hop(chunk, arrivals):
-        arrivals[0].wait_recv()
-        for j in range(2):
-            sums[chunk, 0, j] = (collect(chunk, up_layer, j) + far[chunk, 0, j].astype(F32)).astype(BF16)
-        to_up = move(sums.at[chunk, 0], got.at[chunk, 0], 4 * chunk + 2, up)
-        arrivals[1].wait_recv()
-        for j in range(2):
-            sums[chunk, 1, 2 + j] = (collect(chunk, down_layer, 2 + j) + far[chunk, 1, j].astype(F32)).astype(BF16)
-        to_down = move(sums.at[chunk, 1], got.at[chunk, 1], 4 * chunk + 3, down)
-        return to_up, to_down
-
-    def finish(chunk, arrivals):
-        for c in arrivals:
-            c.wait_recv()
-        rows = pl.ds((chunk % 2) * HALF, HALF)
-        for j in range(4):
-            outs[chunk // 2][j, rows] = collect(chunk, layer, j) + (
-                got[chunk, 0, j].astype(F32) + got[chunk, 1, j].astype(F32)
+        for i, (which, device) in enumerate(((far_layer, across), (up_layer, up), (down_layer, down))):
+            for j in range(SLOTS):
+                sums[chunk][i, j] = collect(chunk, which, j).astype(BF16)
+            index = 3 * chunk + i
+            sum_copies.append(
+                remote(sums[chunk].at[i], got[chunk].at[i], sum_send.at[index], sum_recv.at[index], device)
             )
-
-    ready = {0: first_hop(0)}
-    done = {}
-    for chunk in range(1, 4):
-        ready[chunk] = first_hop(chunk)
-        done[chunk - 1] = second_hop(chunk - 1, ready[chunk - 1])
-    done[3] = second_hop(3, ready[3])
-    for chunk in range(4):
-        finish(chunk, done[chunk])
+            sum_copies[-1].start()
+
+    for chunk, (energy, row, rows) in enumerate(CHUNKS):
+        for i in range(3):
+            sum_copies[3 * chunk + i].wait_recv()
+        for j in range(SLOTS):
+            outs[energy][j, pl.ds(row, rows)] = collect(chunk, layer, j) + (
+                got[chunk][0, j].astype(F32) + got[chunk][1, j].astype(F32) + got[chunk][2, j].astype(F32)
+            )
 
     for c in ids_copies + started + part_copies + sum_copies:
         c.wait_send()
@@ -327,25 +275,24 @@
             out_specs=(vmem, vmem),
             scratch_shapes=[
                 pltpu.VMEM((48, BS, BS), BF16),
-                *[pltpu.VMEM((3, NPS + 1, HALF, BS), BF16)] * 4,
+                *[pltpu.VMEM((3, NPS + 1, rows, BS), BF16) for _, _, rows in CHUNKS],
+                *[pltpu.VMEM((3, SLOTS, rows, BS), BF16) for _, _, rows in CHUNKS],
+                *[pltpu.VMEM((3, SLOTS, rows, BS), BF16) for _, _, rows in CHUNKS],
                 pltpu.SMEM((1, NPS), jnp.int32),
                 pltpu.SMEM((1, NPS), F32),
                 pltpu.SMEM((2, 1, NPS), jnp.int32),
                 pltpu.SMEM((3, 16), jnp.int32),
                 pltpu.VMEM((ORDER, ORDER), F32),
-                pltpu.VMEM((4, 3, SLOTS, HALF, BS), BF16),
-                pltpu.VMEM((4, 2, 2, HALF, BS), BF16),
-                pltpu.VMEM((4, 2, SLOTS, HALF, BS), BF16),
                 dma,
                 dma((2,)),
                 dma((20,)),
                 dma((20,)),
                 dma((2,)),
                 dma((2,)),
-                dma((8,)),
-                dma((8,)),
-                dma((16,)),
-                dma((16,)),
+                dma((2 * N_CHUNK,)),
+                dma((2 * N_CHUNK,)),
+                dma((3 * N_CHUNK,)),
+                dma((3 * N_CHUNK,)),
             ],
             compiler_params=pltpu.CompilerParams(
                 collective_id=0, has_side_effects=True, vmem_limit_bytes=48 * 1024 * 1024

time: 44 us -> 40.2 us (0.914)
  Pallas kernels: 42.4 us -> 38.8 us
    pallas_call x1, Pallas kernels: 41.6 us -> 38 us  [step(): pl.pallas_call(functools.partial(kernel, n_slab), out_shape=(pltpu.VMEM(o...]
where the time goes in v3:
time: 40.2 us; the launch traced here: 40.1 us
  Pallas kernels  38.8 us (97%)
  between operations  1.28 us (3%)
    pallas_call x1, Pallas kernels, step(): pl.pallas_call(functools.partial(kernel, n_slab), out_shape=(pltpu.VMEM(o...  38 us
    pallas_call x1, Pallas kernels, step(): pl.pallas_call(write_out, out_shape=(pltpu.HBM(out.shape, F32), pltpu.HBM...  0.81 us

profile of v3, /device:TPU:2, one launch (start us, length us, event | category | flops | bytes accessed | tf_op | source)
XLA Modules:
  0.0 40.1 jit_solution(13324770426554275078)
XLA Ops:
  1.3 38.0 %shard_map.59 = (f32[4,128,128]{2,1,0:T(8,128)S(1)}, f32[4,128,128]{2,1,0:T(8,128)S(1)}) custom-call(bf16[4,128,128]{2,1,0:T(8,128)(2,1)} %hb_ref.1, s32[1,10]{1,0:T(1,128)} %ids_hbm.1, f32[1,10]{1,0:T(1,128)} %w_hbm.1, f32[1]{0:T(128)S(6)} %copy.6.mu_ref), custom_call_target="tpu_custom_call" | custom-call | tf_op jit(solution)/shard_map/pallas_call | solution.py:271
  39.3 0.8 %shard_map.60 = (f32[4,128,128]{2,1,0:T(8,128)}, f32[4,128,128]{2,1,0:T(8,128)}) custom-call(f32[4,128,128]{2,1,0:T(8,128)S(1)} %get-tuple-element.4.dens_ref, f32[4,128,128]{2,1,0:T(8,128)S(1)} %get-tuple-element.5.energy_ref), custom_call_target="tpu_custom_call" | custom-call | tf_op jit(solution)/shard_map/pallas_call | solution.py:301

commit v4 on v3

--- a/solution.py
+++ b/solution.py
@@ -31,6 +31,15 @@
     r = lax.broadcasted_iota(jnp.int32, (order, order), 0)
     c = lax.broadcasted_iota(jnp.int32, (order, order), 1)
     return jnp.where(r == c, value, 0.0)
+
+
+def mean_square(m, n):
+    total = jnp.zeros((BS, BS), F32)
+    for a in range(NB):
+        for b in range(NB):
+            s, t = slice(a * BS, (a + 1) * BS), slice(b * BS, (b + 1) * BS)
+            total += m[s, t] * n[s, t]
+    return jnp.sum(total, keepdims=True) * (1.0 / ORDER)
 
 
 def mean_diagonal(m):
@@ -92,14 +101,15 @@
         at = piece(group, which_layer, first, count)
         remote(at, at, gather_send.at[index], gather_recv.at[index], up).wait_recv()
 
-    send(hb_ref.at[pl.ds(0, 2)], 0, layer, 0, 2, 0, up)
-    send(hb_ref.at[pl.ds(2, 2)], 0, layer, 2, 2, 1, down)
-    send(hb_ref, 2, layer, 0, 4, 2, other)
-    send(hb_ref.at[pl.ds(2, 2)], 0, layer, 2, 2, 3, up)
-    send(hb_ref.at[pl.ds(0, 2)], 0, layer, 0, 2, 4, down)
-    send(hb_ref, 1, layer, 0, 4, 5, partner)
-    send(hb_ref.at[pl.ds(0, 2)], 0, layer, 0, 2, 6, across)
-    send(hb_ref.at[pl.ds(2, 2)], 0, layer, 2, 2, 7, across)
+    locals_[0].wait()
+    send(piece(0, layer, 0, 2), 0, layer, 0, 2, 0, up)
+    send(piece(0, layer, 2, 2), 0, layer, 2, 2, 1, down)
+    send(piece(0, layer, 0, 4), 2, layer, 0, 4, 2, other)
+    send(piece(0, layer, 2, 2), 0, layer, 2, 2, 3, up)
+    send(piece(0, layer, 0, 2), 0, layer, 0, 2, 4, down)
+    send(piece(0, layer, 0, 4), 1, layer, 0, 4, 5, partner)
+    send(piece(0, layer, 0, 2), 0, layer, 0, 2, 6, across)
+    send(piece(0, layer, 2, 2), 0, layer, 2, 2, 7, across)
     ids_copies = []
     for j, device in enumerate((partner, other)):
         ids_copies.append(remote(ids_hbm, remote_ids.at[j], ids_send.at[j], ids_recv.at[j], device))
@@ -118,7 +128,7 @@
         send(piece(0, which, first, 2), 2, which, first, 2, 8 + i, other)
         send(piece(0, which, first, 2), 1, which, first, 2, 14 + i, partner)
 
-    for c in locals_:
+    for c in locals_[1:]:
         c.wait()
     for c in ids_copies:
         c.wait_recv()
@@ -146,13 +156,13 @@
         request = ids_ref[0, k]
         its_slab = request // 16
         group = jnp.where(its_slab == slab, 0, jnp.where(its_slab == partner_slab, 1, 2))
-        block = near[group * 16 + request - its_slab * 16].astype(F32)
+        block = near[group * 16 + request - its_slab * 16]
         ra, rb = pl.ds(a * BS, BS), pl.ds(b * BS, BS)
         if a == b:
-            h_mat[ra, ra] = block + block.T
+            h_mat[ra, ra] = block.astype(F32) + block.T.astype(F32)
         else:
-            h_mat[ra, rb] = block
-            h_mat[rb, ra] = block.T
+            h_mat[ra, rb] = block.astype(F32)
+            h_mat[rb, ra] = block.T.astype(F32)
     h = h_mat[...]
     mu = mu_ref[0]
     norm2 = jnp.zeros((BS, BS), F32)
@@ -168,12 +178,12 @@
     x0 = mu * inv
     s0 = (inv * inv) * mm(hb, hb) - (2.0 * x0 * inv) * h + eye(ORDER, x0 * x0 - 0.25)
     x1 = (-1.375 * inv) * h - (0.5 * x0) * s0 + (0.5 * inv) * mm(hb, s0.astype(BF16)) + eye(ORDER, 1.375 * x0)
-    t1 = mean_diagonal(x1)
+    t1 = 1.375 * (x0 - inv * mean_diagonal(h)) - (0.5 * x0) * mean_diagonal(s0) + (0.5 * inv) * mean_square(h, s0)
     b1 = x1 - eye(ORDER, t1)
     b1h = b1.astype(BF16)
-    s1 = mm(b1h, b1h) + (2.0 * t1) * b1 + eye(ORDER, t1 * t1)
-    u1 = mean_diagonal(s1)
-    s1 = s1 - eye(ORDER, u1)
+    u0 = mean_square(b1, b1)
+    s1 = mm(b1h, b1h) + (2.0 * t1) * b1 - eye(ORDER, u0)
+    u1 = u0 + t1 * t1
     x2 = (1.5 - 0.5 * u1) * x1 - (0.5 * t1) * s1 - 0.5 * mm(b1h, s1.astype(BF16))
 
     weights = [0.5 * w_ref[0, k] for k in range(NPS)]

time: 40.2 us -> 39.8 us (0.990)
    pallas_call x1, Pallas kernels: 38 us -> 37.6 us  [step(): pl.pallas_call(functools.partial(kernel, n_slab), out_shape=(pltpu.VMEM(o...]
where the time goes in v4:
time: 39.8 us; the launch traced here: 39.7 us
  Pallas kernels  38.4 us (96%)
  between operations  1.28 us (3%)
    pallas_call x1, Pallas kernels, step(): pl.pallas_call(functools.partial(kernel, n_slab), out_shape=(pltpu.VMEM(o...  37.6 us
    pallas_call x1, Pallas kernels, step(): pl.pallas_call(write_out, out_shape=(pltpu.HBM(out.shape, F32), pltpu.HBM...  0.81 us

profile of v4, /device:TPU:2, one launch (start us, length us, event | category | flops | bytes accessed | tf_op | source)
XLA Modules:
  0.0 39.7 jit_solution(17061204533878461639)
XLA Ops:
  1.3 37.6 %shard_map.59 = (f32[4,128,128]{2,1,0:T(8,128)S(1)}, f32[4,128,128]{2,1,0:T(8,128)S(1)}) custom-call(bf16[4,128,128]{2,1,0:T(8,128)(2,1)} %hb_ref.1, s32[1,10]{1,0:T(1,128)} %ids_hbm.1, f32[1,10]{1,0:T(1,128)} %w_hbm.1, f32[1]{0:T(128)S(6)} %copy.6.mu_ref), custom_call_target="tpu_custom_call" | custom-call | tf_op jit(solution)/shard_map/pallas_call | solution.py:281
  38.8 0.8 %shard_map.60 = (f32[4,128,128]{2,1,0:T(8,128)}, f32[4,128,128]{2,1,0:T(8,128)}) custom-call(f32[4,128,128]{2,1,0:T(8,128)S(1)} %get-tuple-element.4.dens_ref, f32[4,128,128]{2,1,0:T(8,128)S(1)} %get-tuple-element.5.energy_ref), custom_call_target="tpu_custom_call" | custom-call | tf_op jit(solution)/shard_map/pallas_call | solution.py:311

commit v5 on v4

--- a/solution.py
+++ b/solution.py
@@ -14,6 +14,7 @@
 ORDER = 512
 SLOTS = 4
 ROWS = 32
+AFTER = 1
 CHUNKS = tuple((energy, row, ROWS) for energy in range(2) for row in range(0, BS, ROWS))
 N_CHUNK = len(CHUNKS)
 MESH = pl.DeviceIdType.MESH
@@ -55,8 +56,8 @@
 
 def kernel(n_slab, hb_ref, ids_hbm, w_hbm, mu_ref, dens_ref, energy_ref, near, *rest):
     parts, sums, got = (rest[i * N_CHUNK : (i + 1) * N_CHUNK] for i in range(3))
-    ids_ref, w_ref, remote_ids, inverse, h_mat, local_sem, small_sem = rest[3 * N_CHUNK : 3 * N_CHUNK + 7]
-    gather_send, gather_recv, ids_send, ids_recv, part_send, part_recv, sum_send, sum_recv = rest[3 * N_CHUNK + 7 :]
+    ids_ref, w_ref, remote_ids, inverse, h_mat, joined, local_sem, small_sem = rest[3 * N_CHUNK : 3 * N_CHUNK + 8]
+    gather_send, gather_recv, ids_send, ids_recv, part_send, part_recv, sum_send, sum_recv = rest[3 * N_CHUNK + 8 :]
     outs = (dens_ref, energy_ref)
     slab = lax.axis_index("slab")
     layer = lax.axis_index("layer")
@@ -75,8 +76,13 @@
         )
 
     barrier = pltpu.get_barrier_semaphore()
-    for device in (other, up, down, partner, across):
+    for device in (up, down, partner, across):
         pl.semaphore_signal(barrier, inc=1, device_id=device, device_id_type=MESH)
+
+    @pl.when(core == 0)
+    def _():
+        pl.semaphore_signal(barrier, inc=1, device_id=other, device_id_type=MESH)
+
     locals_ = [pltpu.make_async_copy(hb_ref, near.at[pl.ds(layer * SLOTS, SLOTS)], local_sem)]
     for i, (src, dst) in enumerate(((ids_hbm, ids_ref), (w_hbm, w_ref))):
         locals_.append(pltpu.make_async_copy(src, dst, small_sem.at[i]))
@@ -85,7 +91,12 @@
     for (_, _, rows), part in zip(CHUNKS, parts):
         for j in range(3):
             part[j, NO_PART] = jnp.zeros((rows, BS), BF16)
-    pl.semaphore_wait(barrier, 5)
+    pl.semaphore_wait(barrier, 4 + core)
+
+    @pl.when(core == 1)
+    def _():
+        pl.semaphore_signal(joined, inc=1, device_id=other, device_id_type=MESH)
+
 
     def piece(group, which_layer, first, count):
         return near.at[pl.ds(group * 16 + which_layer * SLOTS + first, count)]
@@ -104,16 +115,25 @@
     locals_[0].wait()
     send(piece(0, layer, 0, 2), 0, layer, 0, 2, 0, up)
     send(piece(0, layer, 2, 2), 0, layer, 2, 2, 1, down)
-    send(piece(0, layer, 0, 4), 2, layer, 0, 4, 2, other)
+    own_to_other = remote(
+        piece(0, layer, 0, 4), piece(2, layer, 0, 4), gather_send.at[2], gather_recv.at[2], other
+    )
+    started.append(own_to_other)
+
+    @pl.when(core == 1)
+    def _():
+        own_to_other.start()
+
     send(piece(0, layer, 2, 2), 0, layer, 2, 2, 3, up)
     send(piece(0, layer, 0, 2), 0, layer, 0, 2, 4, down)
     send(piece(0, layer, 0, 4), 1, layer, 0, 4, 5, partner)
     send(piece(0, layer, 0, 2), 0, layer, 0, 2, 6, across)
     send(piece(0, layer, 2, 2), 0, layer, 2, 2, 7, across)
-    ids_copies = []
-    for j, device in enumerate((partner, other)):
-        ids_copies.append(remote(ids_hbm, remote_ids.at[j], ids_send.at[j], ids_recv.at[j], device))
-        ids_copies[-1].start()
+    ids_copies = [
+        remote(ids_hbm, remote_ids.at[j], ids_send.at[j], ids_recv.at[j], device)
+        for j, device in enumerate((partner, other))
+    ]
+    ids_copies[0].start()
 
     relays = (
         (down_layer, 0, 0),
@@ -125,8 +145,17 @@
     )
     for i, (which, first, index) in enumerate(relays):
         wait_recv(0, which, first, 2, index)
-        send(piece(0, which, first, 2), 2, which, first, 2, 8 + i, other)
         send(piece(0, which, first, 2), 1, which, first, 2, 14 + i, partner)
+        if i == AFTER:
+
+            @pl.when(core == 0)
+            def _():
+                pl.semaphore_wait(joined, 1)
+                own_to_other.start()
+
+            ids_copies[1].start()
+        for k in range(i + 1) if i == AFTER else [i] if i > AFTER else []:
+            send(piece(0, relays[k][0], relays[k][1], 2), 2, relays[k][0], relays[k][1], 2, 8 + k, other)
 
     for c in locals_[1:]:
         c.wait()
@@ -293,6 +322,7 @@
                 pltpu.SMEM((2, 1, NPS), jnp.int32),
                 pltpu.SMEM((3, 16), jnp.int32),
                 pltpu.VMEM((ORDER, ORDER), F32),
+                pltpu.SemaphoreType.REGULAR,
                 dma,
                 dma((2,)),
                 dma((20,)),

time: 39.8 us -> 39 us (0.980)
  Pallas kernels: 38.4 us -> 37.6 us
    pallas_call x1, Pallas kernels: 37.6 us -> 36.8 us  [step(): pl.pallas_call(functools.partial(kernel, n_slab), out_shape=(pltpu.VMEM(o...]
where the time goes in v5:
time: 39 us; the launch traced here: 38.9 us
  Pallas kernels  37.6 us (96%)
  between operations  1.28 us (3%)
    pallas_call x1, Pallas kernels, step(): pl.pallas_call(functools.partial(kernel, n_slab), out_shape=(pltpu.VMEM(o...  36.8 us
    pallas_call x1, Pallas kernels, step(): pl.pallas_call(write_out, out_shape=(pltpu.HBM(out.shape, F32), pltpu.HBM...  0.81 us

profile of v5, /device:TPU:2, one launch (start us, length us, event | category | flops | bytes accessed | tf_op | source)
XLA Modules:
  0.0 38.9 jit_solution(4433389621725074318)
XLA Ops:
  1.3 36.8 %shard_map.59 = (f32[4,128,128]{2,1,0:T(8,128)S(1)}, f32[4,128,128]{2,1,0:T(8,128)S(1)}) custom-call(bf16[4,128,128]{2,1,0:T(8,128)(2,1)} %hb_ref.1, s32[1,10]{1,0:T(1,128)} %ids_hbm.1, f32[1,10]{1,0:T(1,128)} %w_hbm.1, f32[1]{0:T(128)S(6)} %copy.6.mu_ref), custom_call_target="tpu_custom_call" | custom-call | tf_op jit(solution)/shard_map/pallas_call | solution.py:310
  38.1 0.8 %shard_map.60 = (f32[4,128,128]{2,1,0:T(8,128)}, f32[4,128,128]{2,1,0:T(8,128)}) custom-call(f32[4,128,128]{2,1,0:T(8,128)S(1)} %get-tuple-element.4.dens_ref, f32[4,128,128]{2,1,0:T(8,128)S(1)} %get-tuple-element.5.energy_ref), custom_call_target="tpu_custom_call" | custom-call | tf_op jit(solution)/shard_map/pallas_call | solution.py:341

commit v6 on v5

--- a/solution.py
+++ b/solution.py
@@ -213,7 +213,10 @@
     u0 = mean_square(b1, b1)
     s1 = mm(b1h, b1h) + (2.0 * t1) * b1 - eye(ORDER, u0)
     u1 = u0 + t1 * t1
-    x2 = (1.5 - 0.5 * u1) * x1 - (0.5 * t1) * s1 - 0.5 * mm(b1h, s1.astype(BF16))
+    s1h = s1.astype(BF16)
+
+    def rows_of(m, row, rows):
+        return jnp.concatenate([m[a * BS + row : a * BS + row + rows] for a in range(NB)], axis=0)
 
     weights = [0.5 * w_ref[0, k] for k in range(NPS)]
     part_copies = []
@@ -221,7 +224,7 @@
     def store_parts(matrix, chunk):
         energy, row, rows = CHUNKS[chunk]
         for k, (a, b) in enumerate(PAIRS):
-            first = a * BS + row
+            first = a * BS + row if energy else a * rows
             block = matrix[first : first + rows, b * BS : (b + 1) * BS]
             if not energy and a == b:
                 r = lax.broadcasted_iota(jnp.int32, (rows, BS), 0) + row
@@ -239,9 +242,14 @@
             c.start()
             part_copies.append(c)
 
-    for chunk in range(N_CHUNK):
-        if not CHUNKS[chunk][0]:
-            store_parts(x2, chunk)
+    strips = []
+    for chunk, (energy, row, rows) in enumerate(CHUNKS):
+        if not energy:
+            strip = (1.5 - 0.5 * u1) * rows_of(x1, row, rows) - (0.5 * t1) * rows_of(s1, row, rows)
+            strip = strip - 0.5 * mm(rows_of(b1h, row, rows), s1h)
+            store_parts(strip, chunk)
+            strips.append((rows, strip))
+    x2 = jnp.concatenate([m[a * r : (a + 1) * r] for a in range(NB) for r, m in strips], axis=0)
 
     t2 = mean_diagonal(x2)
     c2 = x2 - eye(ORDER, t2)

time: 39 us -> 38.8 us (level)
  no operation moved by 1% of the time
where the time goes in v6:
time: 38.8 us; the launch traced here: 38.7 us
  Pallas kernels  37.4 us (96%)
  between operations  1.28 us (3%)
    pallas_call x1, Pallas kernels, step(): pl.pallas_call(functools.partial(kernel, n_slab), out_shape=(pltpu.VMEM(o...  36.6 us
    pallas_call x1, Pallas kernels, step(): pl.pallas_call(write_out, out_shape=(pltpu.HBM(out.shape, F32), pltpu.HBM...  0.81 us

profile of v6, /device:TPU:2, one launch (start us, length us, event | category | flops | bytes accessed | tf_op | source)
XLA Modules:
  0.0 38.7 jit_solution(2213402396955435764)
XLA Ops:
  1.3 36.6 %shard_map.59 = (f32[4,128,128]{2,1,0:T(8,128)S(1)}, f32[4,128,128]{2,1,0:T(8,128)S(1)}) custom-call(bf16[4,128,128]{2,1,0:T(8,128)(2,1)} %hb_ref.1, s32[1,10]{1,0:T(1,128)} %ids_hbm.1, f32[1,10]{1,0:T(1,128)} %w_hbm.1, f32[1]{0:T(128)S(6)} %copy.6.mu_ref), custom_call_target="tpu_custom_call" | custom-call | tf_op jit(solution)/shard_map/pallas_call | solution.py:318
  37.9 0.8 %shard_map.60 = (f32[4,128,128]{2,1,0:T(8,128)}, f32[4,128,128]{2,1,0:T(8,128)}) custom-call(f32[4,128,128]{2,1,0:T(8,128)S(1)} %get-tuple-element.4.dens_ref, f32[4,128,128]{2,1,0:T(8,128)S(1)} %get-tuple-element.5.energy_ref), custom_call_target="tpu_custom_call" | custom-call | tf_op jit(solution)/shard_map/pallas_call | solution.py:349
